TPU v7x, 32 devices: a whole 2x2x4 slice. The times are simulated.
32 devices in a mesh: dp: 16 (over z, y, core), mp: 2 (over x).
Axes of the slice: x: 2, y: 2, z: 4, core: 2. Of those that a mesh axis runs over, the one named last changes fastest.
Arguments:
- inputs: bfloat16 [64, 320, 1024], P('dp', 'mp'), may hold values from -6 to 6
- teacher: bfloat16 [64, 320, 1024], P('dp', 'mp'), may hold values from -6 to 6
- keep_mask: int32 [64, 320], P('dp'), may hold values from 0 to 1, as said below
- gain_attn: bfloat16 [1024], P('dp'), may hold values from 0.099609375 to 1.8984375
- qkv_weight: bfloat16 [1024, 3, 1024], P('dp', None, 'mp'), may hold values from -0.25 to 0.25
- out_weight: bfloat16 [1024, 1024], P('dp', 'mp'), may hold values from -0.5 to 0.5
- gain_mlp: bfloat16 [1024], P('dp'), may hold values from 0.099609375 to 1.8984375
- up_weight: bfloat16 [1024, 4096], P('dp', 'mp'), may hold values from -0.1875 to 0.1875
- down_weight: bfloat16 [1024, 4096], P('dp', 'mp'), may hold values from -0.125 to 0.125
Outputs:
- output: bfloat16 [64, 320, 1024], P('dp', 'mp')
- loss: float32 [], replicated
- input_grad: float32 [64, 320, 1024], P('dp', 'mp')
- gain_attn_grad: float32 [1024], P('dp')
- qkv_grad: float32 [1024, 3, 1024], P('dp', None, 'mp')
- out_grad: float32 [1024, 1024], P('dp', 'mp')
- gain_mlp_grad: float32 [1024], P('dp')
- up_grad: float32 [1024, 4096], P('dp', 'mp')
- down_grad: float32 [1024, 4096], P('dp', 'mp')
Inputs may be any that keep to these rules, and one draw needn't show every extreme that they name: `keep_mask`: the first 64 positions of every image are 1; how many of its other positions an image keeps varies from image to image and from draw to draw.
All inputs are finite; a program needn't handle non-finite values.
Results may differ from a plain program's by a relative error of at most 0.009.
The roundings to bfloat16 on the way count: a program that leaves them out, or rounds other values in their place, can miss the bound.
Values may be sent and summed in bfloat16 or wider, within the bound.
A program may use at most 96 MiB of HBM per device.

v0:
```python
import functools
import jax
import jax.numpy as jnp
from jax import lax
from jax.experimental import pallas as pl
from jax.experimental.pallas import tpu as pltpu
from jax.sharding import PartitionSpec as P

MESH = pl.DeviceIdType.MESH
HDIM = 64
CW = 256
EPS = 1e-06
F32 = jnp.float32
BF = jnp.bfloat16
PIECES = 5
BOTH_X = (0, 1, 2, 3, 4, 8, 10, 12, 14, 17)
Z_LAST = (6, 9, 16)
X_WITH = (0, 1, 2, 3, 4)
T_WITH = (10, 12, 14, 15, 17)
FWD_CALLS = (
    (0, 0, 0), (0, 0, 0), (0, 0), (1, 0, 1, 0, 1, 0, 2, 1, 0, 1, 0, 2, 3, 1, 1, 0, 0, 4, 2, 1, 0, 3, 4, 2, 1, 0), (3,), (2,),
    (4, 1), (), (), (), (3, 2, 2, 2, 0), (1, 1, 1),
    (4, 3, 2, 0, 0, 0), (2, 1), (), (4,), (3, 1, 0, 0, 4), (),
    (3, 3), (2, 2), (4, 1, 1), (), (4,), (3, 0),
    (2, 2), (4,), (1, 1), (2, 2, 1, 1, 3, 3, 3, 3, 4), (), (4,),
    (2,), (4,), (3, 1), (4,), (3,), (4,),
    (2, 2, 2), (4,), (2, 2, 1, 1), (3, 4), (), (2,),
    (3,), (3, 2, 3, 4), (3, 4), (3, 4), (3, 4), (4,),
    (3, 4), (3, 4), (4,),
)
NT = (((1,), (1,)), ((), ()))
NN = (((1,), (0,)), ((), ()))


def dot(a, b, dims=NN):
    return lax.dot_general(a, b, dims, preferred_element_type=F32)


class Place:
    def __init__(self, groups):
        self.groups = groups
        dp = lax.axis_index("dp")
        self.x = lax.axis_index("mp")
        self.c = lax.rem(dp, 2)
        self.y = lax.rem(dp // 2, 2)
        self.z = dp // 4

    def at(self, z, y, c, x):
        return {"dp": (z * 2 + y) * 2 + c, "mp": x}

    def far(self, j):
        return self.at(lax.rem(self.z + j, self.groups), self.y, self.c, self.x)

    def over_x(self):
        return self.at(self.z, self.y, self.c, 1 - self.x)

    def over_y(self):
        return self.at(self.z, 1 - self.y, self.c, self.x)

    def over_c(self):
        return self.at(self.z, self.y, 1 - self.c, self.x)

    def partners(self):
        return [self.far(j) for j in range(1, self.groups)] + [
            self.over_x(), self.over_y(), self.over_c()
        ]


def meet(place):
    barrier = pltpu.get_barrier_semaphore()
    partners = place.partners()
    for partner in partners:
        pl.semaphore_signal(barrier, 1, device_id=partner, device_id_type=MESH)
    pl.semaphore_wait(barrier, len(partners))


def member(k, numbers):
    if isinstance(k, int):
        return k in numbers
    found = False
    for n in numbers:
        found = (k == n) | found
    return found


def pick(table, index):
    value = jnp.int32(table[0])
    for n in range(1, len(table)):
        if table[n] != table[n - 1]:
            value = jnp.where(index >= n, table[n], value)
    return value


def when(cond, body):
    if isinstance(cond, bool):
        if cond:
            body()
    else:
        pl.when(cond)(body)


def fwd_kernel(cfg, xin, tin, wq, wo, wu, wd, gain_a, gain_m, mask, *refs):
    (wg_o, at_o, proj_o, lse_o, o_o, h_o, bnt_o, g_o, gp_o, gy_o, gm_o, gmt_o, out_o, xs_o, ts_o, sm_o, loss_o,
     wg, xs, ts, sm, own_sm, kpad, kcol, a, proj, o, lse, h, bn, g, gp, zb, y, tb,
     local_sem, send_sem, recv_sem, extra_send, extra_recv, piece_send, piece_recv, out_sem, misc_sem) = refs
    H, R = cfg["groups"], cfg["rows"]
    NQ, NO, NF = cfg["nq"], cfg["no"], cfg["nf"]
    NCH = NQ + NO + 2 * NF
    IMG, SEQ, D = xs.shape
    HALF = SEQ // 2
    TOK = IMG * SEQ
    GRP = NQ // 3
    place = Place(H)
    x, yy, z, c = place.x, place.y, place.z, place.c
    scale = HDIM ** (-0.5)

    def remote(ref, k, i, device):
        return pltpu.make_async_remote_copy(
            ref, ref, send_sem.at[k, i], recv_sem.at[k, i], device_id=device, device_id_type=MESH
        )

    def source(k):
        if k < NQ:
            return wq.at[k % 3, :, pl.ds((k // 3) * CW, CW)]
        if k < NQ + NO:
            return wo.at[:, pl.ds(CW * (k - NQ), CW)]
        if k < NQ + NO + NF:
            return wu.at[:, pl.ds(CW * (k - NQ - NO), CW)]
        return wd.at[:, pl.ds(CW * (k - NQ - NO - NF), CW)]

    def own(k):
        return pltpu.make_async_copy(source(k), wg.at[k, x, z, yy, c], local_sem.at[k])

    def own_wait(k):
        pltpu.make_async_copy(wq.at[0, :, pl.ds(0, CW)], wg.at[k, x, z, yy, c], local_sem.at[k]).wait()

    def relay(k):
        both = member(k, BOTH_X)
        first = jnp.where(both, 1, 1 - c) if not isinstance(both, bool) else (1 if both else 1 - c)
        xa = jnp.where(first == 1, 1 - x, x)
        ya = jnp.where(first == 1, yy, 1 - yy)
        return xa, ya, jnp.where(first == 1, x, 1 - x), jnp.where(first == 1, 1 - yy, yy)

    def either(k, late, early):
        last = member(k, Z_LAST)
        if isinstance(last, bool):
            (late if last else early)()
        else:
            pl.when(last)(late)
            pl.when(jnp.logical_not(last))(early)

    def s1(k):
        own_wait(k)
        own_block = wg.at[k, x, z, yy, c]
        xa, ya, xb, yb = relay(k)

        def late():
            remote(own_block, k, H - 1, place.at(z, ya, c, xa)).start()
            remote(own_block, k, H, place.at(z, yb, c, xb)).start()

        def early():
            for j in range(1, H):
                remote(own_block, k, j - 1, place.far(j)).start()

        either(k, late, early)

    def s2(k):
        xa, ya, xb, yb = relay(k)

        def late():
            block = wg.at[k, xa, z, ya, c]
            remote(block, k, H - 1, place.at(z, ya, c, xa)).wait_recv()
            remote(block, k, H + 1, place.at(z, yb, c, xb)).start()

        def early():
            for j in range(1, H):
                remote(wg.at[k, x, lax.rem(z + H - j, H), yy, c], k, j - 1, place.far(j)).wait_recv()
            piece_at(k)
            remote(wg.at[k, x, :, yy, c], k, H - 1, place.at(z, ya, c, xa)).start()
            remote(wg.at[k, x, :, yy, c], k, H, place.at(z, yb, c, xb)).start()

        either(k, late, early)

    def s3(k):
        xa, ya, xb, yb = relay(k)

        def late():
            remote(wg.at[k, xb, z, yb, c], k, H, place.at(z, yb, c, xb)).wait_recv()
            remote(wg.at[k, 1 - x, z, 1 - yy, c], k, H + 1, place.at(z, yb, c, xb)).wait_recv()
            for j in range(1, H):
                remote(wg.at[k, :, z, :, c], k, j - 1, place.far(j)).start()

        def early():
            remote(wg.at[k, xa, :, ya, c], k, H - 1, place.at(z, ya, c, xa)).wait_recv()
            remote(wg.at[k, xa, :, ya, c], k, H + 1, place.at(z, yb, c, xb)).start()

        either(k, late, early)

    def s4(k):
        xa, ya, xb, yb = relay(k)

        def late():
            for j in range(1, H):
                remote(wg.at[k, :, lax.rem(z + H - j, H), :, c], k, j - 1, place.far(j)).wait_recv()

        def early():
            remote(wg.at[k, xb, :, yb, c], k, H, place.at(z, yb, c, xb)).wait_recv()
            remote(wg.at[k, 1 - x, :, 1 - yy, c], k, H + 1, place.at(z, yb, c, xb)).wait_recv()

        either(k, late, early)
        remote(wg.at[k, :, :, :, c], k, H + 2, place.over_c()).start()

    def keep_chunk(k):
        return pltpu.make_async_copy(wg.at[k], wg_o.at[k], out_sem.at[k])

    def s5(k):
        remote(wg.at[k, :, :, :, 1 - c], k, H + 2, place.over_c()).wait_recv()
        keep_chunk(k).start()

    PR = HALF // PIECES

    def piece(i, n, to):
        src, dst = ((xin, xs), (tin, ts))[i]
        return pltpu.make_async_remote_copy(
            src.at[pl.ds(IMG * (1 - x), IMG), pl.ds(PR * n, PR)], dst.at[:, pl.ds(HALF * to + PR * n, PR)],
            piece_send.at[i, n], piece_recv.at[i, n], device_id=place.over_x(), device_id_type=MESH
        )

    def piece_at(k):
        for i, chunks in enumerate((X_WITH, T_WITH)):
            for n, chunk_no in enumerate(chunks):
                when(k == chunk_no, lambda i=i, n=n: piece(i, n, x).start())

    def pieces_in(i):
        for n in range(PIECES):
            piece(i, n, 1 - x).wait_recv()

    stages = (s1, s2, s3, s4, s5)
    pos = [0] * 5
    place_no = [0]

    def upcoming():
        calls = []
        for i in FWD_CALLS[place_no[0]]:
            calls.append((i, pos[i]))
            pos[i] += 1
        place_no[0] += 1
        return calls

    def serve():
        for i, n in upcoming():
            stages[i](n)

    def serve_in(index, calls, starts):
        for i in (4, 3, 2, 1, 0):
            counts = [call.count(i) for call in calls]
            if max(counts):
                first = pick(starts[i], index)

                @pl.loop(first, first + pick(counts, index))
                def _(n, i=i):
                    stages[i](n)

    def served(count):
        calls = FWD_CALLS[place_no[0]:place_no[0] + count]
        place_no[0] += count
        starts = [[pos[i] + sum(call.count(i) for call in calls[:n]) for n in range(count)] for i in range(5)]
        for i in range(5):
            pos[i] += sum(call.count(i) for call in calls)
        return calls, starts

    kept = []

    def keep(src, dst):
        copy = pltpu.make_async_copy(src, dst, misc_sem.at[len(kept)])
        copy.start()
        kept.append(copy)

    def extra(src, dst, i, device):
        return pltpu.make_async_remote_copy(
            src, dst, extra_send.at[i], extra_recv.at[i], device_id=device, device_id_type=MESH
        )

    for k in range(NCH):
        own(k).start()
    mine = pl.ds(HALF * x, HALF)
    xl = pltpu.make_async_copy(xin.at[pl.ds(IMG * x, IMG)], xs.at[:, mine], misc_sem.at[30])
    tl = pltpu.make_async_copy(tin.at[pl.ds(IMG * x, IMG)], ts.at[:, mine], misc_sem.at[31])
    spread = (lax.broadcasted_iota(jnp.int32, (R, D), 1)
              == lax.broadcasted_iota(jnp.int32, (R, D), 0) + lax.axis_index("dp") * R)
    spread = jnp.where(spread, 1.0, 0.0).astype(BF)
    line = lax.broadcasted_iota(jnp.int32, (8, D), 0)
    own_sm[...] = jnp.where(line == 0, dot(gain_a[...], spread),
                            jnp.where(line == 1, dot(gain_m[...], spread),
                                      jnp.sum(mask[...].astype(F32))))
    sl = pltpu.make_async_copy(own_sm, sm.at[z, yy, c], misc_sem.at[29])
    xl.start()
    tl.start()
    sl.start()
    meet(place)
    sl.wait()
    for j in range(1, H):
        extra(sm.at[z, yy, c], sm.at[z, yy, c], 3 + j, place.far(j)).start()
    serve()
    for j in range(1, H):
        extra(sm.at[z, yy, c], sm.at[lax.rem(z + H - j, H), yy, c], 3 + j, place.far(j)).wait_recv()
    extra(sm.at[:, yy, c], sm.at[:, yy, c], 2, place.over_y()).start()
    serve()
    extra(sm.at[:, 1 - yy, c], sm.at[:, 1 - yy, c], 2, place.over_y()).wait_recv()
    extra(sm.at[:, :, c], sm.at[:, :, c], 3, place.over_c()).start()
    kpad[...] = jnp.zeros_like(kpad)
    for i in range(IMG):
        kpad[:, 0:SEQ] = jnp.broadcast_to(mask[pl.ds(IMG * x + i, 1)].astype(F32), (128, SEQ))
        kcol[i] = jnp.transpose(kpad[...])[0:SEQ]
    serve()
    extra(sm.at[:, :, 1 - c], sm.at[:, :, 1 - c], 3, place.over_c()).wait_recv()
    totals = jnp.sum(sm[...].reshape(H * 4, 8, D), axis=0)
    sm_o[...] = totals
    xl.wait()
    serve()
    pieces_in(0)
    keep(xs, xs_o)

    RB = 32

    def rows_of(ref, r):
        per = SEQ // RB
        return ref[r // per, pl.ds(pl.multiple_of(lax.rem(r, per) * RB, RB), RB)]

    def norm_to(values, gain):
        centre = values - jnp.mean(values, axis=-1, keepdims=True)
        spread = jnp.mean(centre * centre, axis=-1, keepdims=True)
        return (centre * lax.rsqrt(spread + EPS) * gain).astype(BF)

    for part in range(2):
        count = TOK // RB // 2

        @pl.loop(part * count, (part + 1) * count)
        def _(r):
            a[pl.ds(pl.multiple_of(r * RB, RB), RB)] = norm_to(rows_of(xs, r).astype(F32), sm_o[0:1])

        serve()

    def transposed(src, dst):
        @pl.loop(0, D // 128)
        def _(d):
            t = jnp.transpose(src[:, pl.ds(pl.multiple_of(d * 128, 128), 128)].astype(F32))
            t = t.reshape(64 // R, 2, R, TOK)
            for p in range(2):
                dst[p, pl.ds(pl.multiple_of(d * 64, 64), 64)] = t[:, p].reshape(64, TOK).astype(BF)

    transposed(a, tb)
    keep(tb, at_o)
    serve()

    def chunk(k, half):
        return wg[k, half].reshape(D, CW)

    def project(k):
        @pl.loop(0, 2)
        def _(half):
            proj[k, half] = dot(a[...], chunk(k, half)).astype(BF).reshape(IMG, SEQ, CW)

    lane = lax.broadcasted_iota(jnp.int32, (SEQ, CW), 1) // HDIM

    def attend(group, u):
        half, i = u // IMG, lax.rem(u, IMG)
        q = proj[3 * group, half, i]
        key = proj[3 * group + 1, half, i]
        val = proj[3 * group + 2, half, i]
        allowed = mask[pl.ds(IMG * x + i, 1)] > 0
        total = jnp.zeros((SEQ, CW), F32)
        logs = jnp.zeros((SEQ, 128), F32)
        spot = lax.broadcasted_iota(jnp.int32, (SEQ, 128), 1)
        for head in range(CW // HDIM):
            scores = dot(jnp.where(lane == head, q, 0), key, NT) * scale
            scores = jnp.where(allowed, scores, -1e30)
            top = jnp.max(scores, axis=-1, keepdims=True)
            raised = jnp.exp(scores - top)
            norm = jnp.sum(raised, axis=-1, keepdims=True)
            soft = (raised / norm).astype(BF)
            total = total + dot(soft, jnp.where(lane == head, val, 0))
            logs = jnp.where(spot == head, top + jnp.log(norm), logs)
        o[group, half, i] = total.astype(BF)
        lse[group, half, i] = logs

    for group in range(GRP):
        for k in range(3 * group, 3 * group + 3):
            serve()
            project(k)
        places = served(2 * IMG)

        @pl.loop(0, 2 * IMG)
        def _(u, group=group, places=places):
            serve_in(u, *places)
            attend(group, u)

    keep(proj, proj_o)
    keep(lse, lse_o)
    keep(o, o_o)

    def gathered(src, k, half):
        return src[k, half].reshape(TOK, CW)

    h[...] = xs[...].reshape(TOK, D).astype(F32)
    for k in range(NO):
        serve()

        @pl.loop(0, 2)
        def _(half, k=k):
            h[...] += dot(gathered(o, k, half), chunk(NQ + k, half), NT)

    keep(h, h_o)

    for part in range(2):
        count = TOK // RB // 2
        serve()

        @pl.loop(part * count, (part + 1) * count)
        def _(r):
            at = pl.ds(pl.multiple_of(r * RB, RB), RB)
            bn[at] = norm_to(h[at], sm_o[1:2])

    first_up = NQ + NO

    def gelu(k, half):
        GB = 64

        @pl.loop(0, TOK // GB)
        def _(r):
            at = pl.ds(pl.multiple_of(r * GB, GB), GB)
            v = zb[at]
            cdf = 0.5 * (1.0 + lax.erf(v * 0.7071067811865476))
            g[k, half, at] = (v * cdf).astype(BF)
            gp[k, half, at] = (cdf + v * (jnp.exp(-0.5 * (v * v)) * 0.3989422804014327)).astype(BF)

    for k in range(NF):
        serve()
        calls = upcoming()

        @pl.loop(0, 2)
        def _(half, k=k, calls=calls):
            @pl.when(half == 1)
            def _():
                for i, n in calls:
                    stages[i](n)

            zb[...] = dot(bn[...], chunk(first_up + k, half))
            gelu(k, half)

    keep(g, g_o)
    keep(gp, gp_o)
    first_down = first_up + NF
    kept[1].wait()
    serve()
    transposed(bn, tb)
    keep(tb, bnt_o)
    serve()
    y[...] = h[...]

    for k in range(NF):
        serve()

        @pl.loop(0, 2)
        def _(half, k=k):
            y[...] += dot(g[k, half], chunk(first_down + k, half), NT)

    assert pos == [NCH] * 5 and place_no[0] == len(FWD_CALLS)
    tl.wait()
    pieces_in(1)
    keep(ts, ts_o)
    zb[0:RB, 0:128] = jnp.zeros((RB, 128), F32)
    factor = 2.0 * cfg["tokens"] / sm_o[2:3]
    xs_ref = xs

    for copy in kept[:1]:
        copy.wait()

    @pl.loop(0, TOK // RB)
    def _(r):
        at = pl.ds(pl.multiple_of(r * RB, RB), RB)
        per = SEQ // RB
        img, pos = r // per, pl.multiple_of(lax.rem(r, per) * RB, RB)
        res = y[at]
        kept_rows = jnp.tile(kcol[img, pl.ds(pos, RB)], (1, D // 128))
        xs_ref[img, pl.ds(pos, RB)] = (res * kept_rows).astype(BF)
        error = res - ts[img, pl.ds(pos, RB)].astype(F32)
        squares = error * error * kept_rows
        part = squares[:, 0:128]
        for n in range(1, D // 128):
            part = part + squares[:, n * 128:(n + 1) * 128]
        zb[0:RB, 0:128] += part
        grad = factor * kept_rows * error
        y[at] = grad
        a[at] = grad.astype(BF)

    loss_o[...] = jnp.zeros_like(loss_o) + jnp.sum(zb[0:RB, 0:128]) * (1.0 / D)
    keep(xs, out_o)
    keep(y, gy_o)
    keep(a, gm_o)
    kept[8].wait()
    transposed(a, tb)
    keep(tb, gmt_o)
    for n, copy in enumerate(kept):
        if n not in (0, 1, 8):
            copy.wait()
    for i in range(2):
        for n in range(PIECES):
            piece(i, n, x).wait_send()
    for j in range(1, H):
        extra(sm.at[z, yy, c], sm.at[z, yy, c], 3 + j, place.far(j)).wait_send()
    extra(sm.at[:, yy, c], sm.at[:, yy, c], 2, place.over_y()).wait_send()
    extra(sm.at[:, :, c], sm.at[:, :, c], 3, place.over_c()).wait_send()

    @pl.loop(0, NCH)
    def _(k):
        keep_chunk(k).wait()

        def late():
            for j in range(1, H):
                remote(wg.at[k, :, z, :, c], k, j - 1, place.far(j)).wait_send()
            for i in (H - 1, H, H + 1):
                remote(wg.at[k, x, z, yy, c], k, i, place.over_x()).wait_send()

        def early():
            for j in range(1, H):
                remote(wg.at[k, x, z, yy, c], k, j - 1, place.far(j)).wait_send()
            for i in (H - 1, H, H + 1):
                remote(wg.at[k, x, :, yy, c], k, i, place.over_x()).wait_send()

        either(k, late, early)
        remote(wg.at[k, :, :, :, c], k, H + 2, place.over_c()).wait_send()


def any_spec():
    return pl.BlockSpec(memory_space=pl.ANY)


def vmem_spec():
    return pl.BlockSpec(memory_space=pltpu.VMEM)


def forward(cfg, xin, tin, wq, wo, wu, wd, gain_a, gain_m, mask):
    H, R = cfg["groups"], cfg["rows"]
    NQ, NO, NF = cfg["nq"], cfg["no"], cfg["nf"]
    NCH = NQ + NO + 2 * NF
    IMG = xin.shape[0] // 2
    SEQ, D = 2 * xin.shape[1], xin.shape[2]
    TOK = IMG * SEQ
    GRP = NQ // 3
    wg = (NCH, 2, H, 2, 2, R, CW)
    lhs = (2, D // 2, TOK)
    big = (NF, 2, TOK, CW)
    shapes = [
        (wg, BF), (lhs, BF), ((NQ, 2, IMG, SEQ, CW), BF), ((GRP, 2, IMG, SEQ, 128), F32),
        ((GRP, 2, IMG, SEQ, CW), BF), ((TOK, D), F32), (lhs, BF), (big, BF), (big, BF),
        ((TOK, D), F32), ((TOK, D), BF), (lhs, BF), ((IMG, SEQ, D), BF), ((IMG, SEQ, D), BF), ((IMG, SEQ, D), BF),
        ((8, D), F32), ((8, 128), F32),
    ]
    return pl.pallas_call(
        functools.partial(fwd_kernel, cfg),
        name="gather_forward",
        out_shape=[jax.ShapeDtypeStruct(s, t) for s, t in shapes],
        in_specs=[any_spec()] * 6 + [vmem_spec()] * 3,
        out_specs=[any_spec()] * 15 + [vmem_spec()] * 2,
        scratch_shapes=[
            pltpu.VMEM(wg, BF), pltpu.VMEM((IMG, SEQ, D), BF), pltpu.VMEM((IMG, SEQ, D), BF),
            pltpu.VMEM((H, 2, 2, 8, D), F32), pltpu.VMEM((8, D), F32), pltpu.VMEM((128, -(-SEQ // 128) * 128), F32),
            pltpu.VMEM((IMG, SEQ, 128), F32), pltpu.VMEM((TOK, D), BF),
            pltpu.VMEM((NQ, 2, IMG, SEQ, CW), BF), pltpu.VMEM((GRP, 2, IMG, SEQ, CW), BF),
            pltpu.VMEM((GRP, 2, IMG, SEQ, 128), F32), pltpu.VMEM((TOK, D), F32), pltpu.VMEM((TOK, D), BF),
            pltpu.VMEM(big, BF), pltpu.VMEM(big, BF), pltpu.VMEM((TOK, CW), F32), pltpu.VMEM((TOK, D), F32),
            pltpu.VMEM(lhs, BF),
            pltpu.SemaphoreType.DMA((NCH,)), pltpu.SemaphoreType.DMA((NCH, H + 3)),
            pltpu.SemaphoreType.DMA((NCH, H + 3)), pltpu.SemaphoreType.DMA((H + 4,)),
            pltpu.SemaphoreType.DMA((H + 4,)), pltpu.SemaphoreType.DMA((2, PIECES)),
            pltpu.SemaphoreType.DMA((2, PIECES)), pltpu.SemaphoreType.DMA((NCH,)), pltpu.SemaphoreType.DMA((32,)),
        ],
        compiler_params=pltpu.CompilerParams(
            collective_id=0, has_side_effects=True, vmem_limit_bytes=63 * 2**20
        ),
    )(xin, tin, wq, wo, wu, wd, gain_a, gain_m, mask)


def config(inputs, weights):
    rows = weights[0].shape[0]
    dps = lax.axis_size("dp")
    return {
        "groups": dps // 4,
        "rows": rows,
        "nq": weights[0].shape[1] * weights[0].shape[2] // CW,
        "no": weights[1].shape[1] // CW,
        "nf": weights[2].shape[1] // CW,
        "tokens": float(inputs.shape[0] * inputs.shape[1] * dps * lax.axis_size("mp")),
    }


SLOTS = 3
FAR_AT = 4
WSLOTS = 4
CALLS = (
    (0, 0, 0, 0, 0), (0, 0, 0, 0, 0), (0, 0, 0, 0, 0), (1, 0, 0, 0, 0), (0, 0, 0, 0, 0),
    (1, 0, 0, 0, 0), (0, 0, 0, 0, 0), (1, 0, 0, 0, 0), (0, 1, 0, 0, 0), (1, 0, 0, 0, 0),
    (0, 1, 0, 0, 0), (1, 0, 0, 0, 0), (0, 0, 0, 0, 0), (1, 0, 0, 0, 0), (0, 1, 0, 0, 0),
    (1, 0, 0, 0, 0), (0, 0, 0, 0, 0), (1, 0, 0, 0, 0), (0, 0, 2, 0, 0), (1, 1, 1, 0, 0),
    (1, 0, 0, 0, 0), (0, 0, 0, 0, 0), (0, 0, 0, 0, 0), (1, 1, 0, 1, 0), (0, 0, 0, 0, 0),
    (1, 0, 0, 1, 0), (0, 0, 0, 0, 0), (1, 1, 1, 1, 0), (1, 0, 0, 0, 0), (0, 1, 0, 0, 0),
    (0, 0, 0, 0, 0), (1, 1, 0, 0, 0), (1, 0, 0, 1, 0), (0, 1, 1, 0, 0), (0, 1, 0, 0, 0),
    (0, 0, 0, 0, 0), (0, 0, 0, 0, 0), (1, 0, 0, 0, 0), (0, 1, 0, 0, 0), (1, 0, 3, 1, 0),
    (0, 1, 3, 0, 0), (0, 1, 0, 1, 0), (0, 1, 1, 1, 0), (0, 0, 0, 0, 0), (0, 0, 1, 1, 0),
    (0, 1, 0, 0, 0), (1, 0, 0, 1, 0), (1, 0, 1, 0, 0), (1, 1, 0, 1, 0), (0, 1, 1, 1, 0),
    (0, 0, 1, 1, 0), (0, 1, 1, 1, 0), (0, 1, 0, 2, 0), (0, 0, 0, 0, 0), (0, 1, 1, 1, 0),
    (0, 0, 0, 0, 0), (1, 0, 0, 1, 0), (1, 0, 1, 0, 0), (1, 1, 1, 0, 0), (0, 1, 0, 1, 0),
)
DRAIN = (
    3, 2, 1, 4, 3, 4, 1, 3, 4, 2, 2, 2, 4, 3, 3, 3, 4,
)
OUT_FIRST = 1


def bwd_kernel(cfg, wg, at_i, proj_i, lse_i, o_i, h_i, bnt_i, g_i, gp_i, gy_i, gm_i, gmt_i, out_i, xs_i,
               totals, loss_i, mask, *refs):
    (out_o, ig_o, dq_o, do_o, du_o, dd_o, stat_o,
     q, snd, rcv, near, farr, dw, wb, gb_buf, gpb, gz, zb, gm, lhs1, lhs2, acc, gh, h, o, go, proj, lse, xb, igr, stat, sbuf, zsum,
     core_send, core_recv, credit, near_send, near_recv, far_send, far_recv, extra_send, extra_recv, piece_send, piece_recv,
     wsem, gsem, misc_sem, dw_sem) = refs
    H, R = cfg["groups"], cfg["rows"]
    NQ, NO, NF = cfg["nq"], cfg["no"], cfg["nf"]
    NCH = NQ + NO + 2 * NF
    IMG, SEQ, D = xb.shape
    HALF = SEQ // 2
    TOK = IMG * SEQ
    GRP = NQ // 3
    place = Place(H)
    x, yy, z, c = place.x, place.y, place.z, place.c
    scale = HDIM ** (-0.5)

    def ident(p):
        ff = jnp.where(lax.rem(p, 2) == 0, NQ + NO + NF + p // 2, NQ + NO + p // 2)
        return jnp.where(p < 2 * NF, ff, jnp.where(p < 2 * NF + NO, p - 2 * NF + NQ, p - 2 * NF - NO))

    def relay(p):
        both = (p >= OUT_FIRST) & (p < OUT_FIRST + PIECES)
        first = jnp.where(both, 1, 1 - c)
        xa = jnp.where(first == 1, 1 - x, x)
        ya = jnp.where(first == 1, yy, 1 - yy)
        return xa, ya, jnp.where(first == 1, x, 1 - x), jnp.where(first == 1, 1 - yy, yy)

    loads = []

    def load(src, dst):
        copy = pltpu.make_async_copy(src, dst, misc_sem.at[len(loads)])
        copy.start()
        loads.append(copy)
        return copy

    def wload(n):
        return pltpu.make_async_copy(wg.at[ident(n)], wb.at[lax.rem(n, WSLOTS)], wsem.at[n])

    def gload(j):
        s = lax.rem(j, 2)
        return (pltpu.make_async_copy(g_i.at[j], gb_buf.at[s], gsem.at[j, 0]),
                pltpu.make_async_copy(gp_i.at[j], gpb.at[s], gsem.at[j, 1]))

    gm_l = load(gm_i, gm)
    gmt_l = load(gmt_i, lhs1)
    for j in range(2):
        for copy in gload(jnp.int32(j)):
            copy.start()
    for n in range(WSLOTS):
        wload(jnp.int32(n)).start()
    bnt_l = load(bnt_i, lhs2)
    out_l = load(out_i, xb)
    gy_l = load(gy_i, gh)
    h_l = load(h_i, h)
    o_l = load(o_i, o)
    proj_l = load(proj_i, proj)
    lse_l = load(lse_i, lse)

    def extra(src, dst, i, device):
        return pltpu.make_async_remote_copy(
            src, dst, extra_send.at[i], extra_recv.at[i], device_id=device, device_id_type=MESH
        )

    meet(place)

    def core_copy(p, start=False):
        s = lax.rem(p, SLOTS)
        return pltpu.make_async_remote_copy(
            snd.at[s], rcv.at[s], core_send.at[p], core_recv.at[p], device_id=place.over_c(), device_id_type=MESH
        )

    def near_copy(src, k, i, device):
        return pltpu.make_async_remote_copy(
            src, near.at[k, i], near_send.at[k, i], near_recv.at[k, i], device_id=device, device_id_type=MESH
        )

    def far_copy(k, zd, j):
        return pltpu.make_async_remote_copy(
            q.at[k, x, zd, yy], farr.at[k, j - 1], far_send.at[k, j - 1], far_recv.at[k, j - 1],
            device_id=place.far(j), device_id_type=MESH
        )

    def produce(p, lhs, rhs):
        k = ident(p)
        s = lax.rem(p, SLOTS)
        pl.when(p >= SLOTS)(lambda: core_copy(p - SLOTS).wait_send())

        @pl.loop(0, 2)
        def _(half):
            snd[s, half] = dot(lhs[1 - c], rhs(half)).astype(BF).reshape(H, 2, R, CW)
            q[k, half] = dot(lhs[c], rhs(half)).astype(BF).reshape(H, 2, R, CW)

        pl.when(p >= SLOTS)(lambda: pl.semaphore_wait(credit, 1))
        core_copy(p).start()

    def added(k, xi, yi, others):
        @pl.loop(0, H)
        def _(n):
            total = q[k, xi, n, yi].astype(F32)
            for other in others:
                total = total + near[k, other, n].astype(F32)
            q[k, xi, n, yi] = total.astype(BF)

    def r1(p):
        k = ident(p)
        s = lax.rem(p, SLOTS)
        core_copy(p).wait_recv()

        @pl.loop(0, 2 * H)
        def _(n):
            i, m = n // H, lax.rem(n, H)
            for y2 in range(2):
                q[k, i, m, y2] = (q[k, i, m, y2].astype(F32) + rcv[s, i, m, y2].astype(F32)).astype(BF)

        pl.when(p + SLOTS < NCH)(
            lambda: pl.semaphore_signal(credit, 1, device_id=place.over_c(), device_id_type=MESH)
        )
        xa, ya, xo, yo = relay(p)
        near_copy(q.at[k, 1 - x, :, 1 - yy], k, 0, place.at(z, yo, c, xo)).start()
        near_copy(q.at[k, xo, :, yo], k, 1, place.at(z, yo, c, xo)).start()

    def r2(p):
        k = ident(p)
        xa, ya, xo, yo = relay(p)
        near_copy(q.at[k, 1 - x, :, 1 - yy], k, 0, place.at(z, yo, c, xo)).wait_recv()
        added(k, xa, ya, (0,))
        near_copy(q.at[k, xa, :, ya], k, 2, place.at(z, ya, c, xa)).start()

    def r3(p):
        k = ident(p)
        xa, ya, xo, yo = relay(p)
        near_copy(q.at[k, xo, :, yo], k, 1, place.at(z, yo, c, xo)).wait_recv()
        near_copy(q.at[k, xa, :, ya], k, 2, place.at(z, ya, c, xa)).wait_recv()
        added(k, x, yy, (1, 2))
        for j in range(1, H):
            far_copy(k, lax.rem(z + j, H), j).start()

    def dw_out(k):
        def send(first, count, at):
            @pl.when((k >= first) & (k < first + count))
            def _():
                pltpu.make_async_copy(dw.at[k], at(pl.multiple_of((k - first) * CW, CW)), dw_sem.at[k]).start()

        for part in range(3):
            @pl.when((k < NQ) & (lax.rem(k, 3) == part))
            def _(part=part):
                pltpu.make_async_copy(
                    dw.at[k], dq_o.at[part, :, pl.ds(pl.multiple_of(k // 3 * CW, CW), CW)], dw_sem.at[k]
                ).start()
        send(NQ, NO, lambda n: do_o.at[:, pl.ds(n, CW)])
        send(NQ + NO, NF, lambda n: du_o.at[:, pl.ds(n, CW)])
        send(NQ + NO + NF, NF, lambda n: dd_o.at[:, pl.ds(n, CW)])

    def r4(p):
        k = ident(p)
        total = q[k, x, z, yy].astype(F32)
        for j in range(1, H):
            far_copy(k, lax.rem(z + j, H), j).wait_recv()
            total = total + farr[k, j - 1].astype(F32)
        dw[k] = total
        dw_out(k)

    stages = (r1, r2, r3, r4)

    before = [[sum(call[i] for call in CALLS[:n]) for n in range(len(CALLS) + 1)] for i in range(5)]
    place_no = [0]

    def serve(numbers, index=None):
        for i in (3, 2, 1, 0):
            counts = [CALLS[n][i] for n in numbers]
            starts = [before[i][n] for n in numbers]
            if index is None:
                for n in range(counts[0]):
                    stages[i](jnp.int32(starts[0] + n))
            elif max(counts) == 1:
                pl.when(pick(counts, index) > 0)(lambda i=i, starts=starts: stages[i](pick(starts, index)))
            elif max(counts) > 1:
                first = pick(starts, index)

                @pl.loop(first, first + pick(counts, index))
                def _(n, i=i):
                    stages[i](n)

    def serve_next():
        serve([place_no[0]])
        place_no[0] += 1

    gm_l.wait()
    gmt_l.wait()
    bnt_l.wait()

    def wchunk(n, half):
        return wb[lax.rem(n, WSLOTS), half].reshape(D, CW)

    def wnext(n):
        pl.when(n + WSLOTS < NCH)(lambda: wload(n + WSLOTS).start())

    GB = 64
    PR = HALF // PIECES
    mine = pl.ds(HALF * x, HALF)

    def piece(i, n):
        return pltpu.make_async_remote_copy(
            xb.at[:, pl.ds(HALF * (1 - x) + PR * n, PR)],
            igr.at[:, pl.ds(PR * n, PR)] if i else out_o.at[pl.ds(IMG * x, IMG), pl.ds(PR * n, PR)],
            piece_send.at[i, n], piece_recv.at[i, n], device_id=place.over_x(), device_id_type=MESH
        )

    acc[...] = jnp.zeros_like(acc)
    out_l.wait()
    out_c = pltpu.make_async_copy(xb.at[:, mine], out_o.at[pl.ds(IMG * x, IMG)], misc_sem.at[30])
    out_c.start()

    @pl.loop(0, NF)
    def _(j):
        s = lax.rem(j, 2)
        pl.when(j < PIECES)(lambda: piece(0, j).start())
        gl, gpl = gload(j)
        gl.wait()
        produce(2 * j, lhs1, lambda half: gb_buf[s, half])
        serve([4 * n for n in range(NF)], j)
        gpl.wait()
        wload(2 * j).wait()

        @pl.loop(0, 2)
        def _(half):
            zb[...] = dot(gm[...], wchunk(2 * j, half))

            @pl.loop(0, TOK // GB)
            def _(r):
                at = pl.ds(pl.multiple_of(r * GB, GB), GB)
                gz[half, at] = (zb[at] * gpb[s, half, at].astype(F32)).astype(BF)

        wnext(2 * j)

        @pl.when(j + 2 < NF)
        def _():
            for copy in gload(j + 2):
                copy.start()

        serve([4 * n + 1 for n in range(NF)], j)
        produce(2 * j + 1, lhs2, lambda half: gz[half])
        serve([4 * n + 2 for n in range(NF)], j)
        wload(2 * j + 1).wait()

        @pl.loop(0, 2)
        def _(half):
            acc[...] += dot(gz[half], wchunk(2 * j + 1, half), NT)

        wnext(2 * j + 1)
        serve([4 * n + 3 for n in range(NF)], j)

    place_no[0] = 4 * NF
    RB = 32

    def norm_back(values, grad, gain):
        centre = values - jnp.mean(values, axis=-1, keepdims=True)
        spread = jnp.mean(centre * centre, axis=-1, keepdims=True)
        scaled = lax.rsqrt(spread + EPS)
        unit = centre * scaled
        e = grad * gain
        first = jnp.mean(e, axis=-1, keepdims=True)
        second = jnp.mean(e * unit, axis=-1, keepdims=True)
        return scaled * (e - first - unit * second), grad * unit

    def fold(v):
        return jnp.sum(v.reshape(RB // 8, 8, D), axis=0)

    base = 2 * NF
    stat[...] = jnp.zeros_like(stat)
    gy_l.wait()
    h_l.wait()

    for part in range(2):
        count = TOK // RB // 2

        @pl.loop(part * count, (part + 1) * count)
        def _(r):
            at = pl.ds(pl.multiple_of(r * RB, RB), RB)
            back, product = norm_back(h[at], acc[at], totals[1:2])
            total = gh[at] + back
            gh[at] = total
            gm[at] = total.astype(BF)
            stat[1] += fold(product)

        serve_next()

    def transposed(src, dst):
        @pl.loop(0, D // 128)
        def _(d):
            t = jnp.transpose(src[:, pl.ds(pl.multiple_of(d * 128, 128), 128)].astype(F32))
            t = t.reshape(64 // R, 2, R, TOK)
            for p in range(2):
                dst[p, pl.ds(pl.multiple_of(d * 64, 64), 64)] = t[:, p].reshape(64, TOK).astype(BF)

    at_l = load(at_i, lhs2)
    transposed(gm, lhs1)
    o_l.wait()
    for k in range(NO):
        produce(jnp.int32(base + k), lhs1, lambda half, k=k: o[k, half].reshape(TOK, CW))
        serve_next()
        wload(jnp.int32(base + k)).wait()

        @pl.loop(0, 2)
        def _(half, k=k):
            go[k, half] = dot(gm[...], wchunk(jnp.int32(base + k), half)).astype(BF).reshape(IMG, SEQ, CW)

        wnext(jnp.int32(base + k))
        serve_next()
    proj_l.wait()
    lse_l.wait()
    lane = lax.broadcasted_iota(jnp.int32, (SEQ, CW), 1) // HDIM
    TN = (((0,), (0,)), ((), ()))

    def attend_back(group, u):
        half, i = u // IMG, lax.rem(u, IMG)
        qr, kr, vr = 3 * group, 3 * group + 1, 3 * group + 2
        query, key, val = proj[qr, half, i], proj[kr, half, i], proj[vr, half, i]
        grad = go[group, half, i]
        logs = lse[group, half, i]
        allowed = mask[pl.ds(IMG * x + i, 1)] > 0
        gq = jnp.zeros((SEQ, CW), F32)
        gk = jnp.zeros((SEQ, CW), F32)
        gv = jnp.zeros((SEQ, CW), F32)
        for head in range(CW // HDIM):
            of_head = lane == head
            qm = jnp.where(of_head, query, 0)
            gom = jnp.where(of_head, grad, 0)
            scores = jnp.where(allowed, dot(qm, key, NT) * scale, -1e30)
            soft = jnp.exp(scores - logs[:, head:head + 1])
            gsoft = dot(gom, val, NT)
            inner = jnp.sum(gsoft * soft, axis=-1, keepdims=True)
            gs = (soft * (gsoft - inner)).astype(BF)
            gq = gq + dot(gs, jnp.where(of_head, key, 0))
            gk = gk + dot(gs, qm, TN)
            gv = gv + dot(soft.astype(BF), gom, TN)
        proj[qr, half, i] = (gq * scale).astype(BF)
        proj[kr, half, i] = (gk * scale).astype(BF)
        proj[vr, half, i] = gv.astype(BF)

    acc[...] = jnp.zeros_like(acc)
    at_l.wait()
    out_c.wait()
    for n in range(PIECES):
        piece(0, n).wait_send()
    xs_l = load(xs_i, xb)

    n0 = place_no[0]
    per_group = 2 * IMG + 6
    place_no[0] += per_group * GRP

    def numbers(first, count):
        return [n0 + per_group * group + first + n for group in range(GRP) for n in range(count)]

    @pl.loop(0, GRP)
    def _(group):
        @pl.loop(0, 2 * IMG)
        def _(u):
            serve(numbers(0, 2 * IMG), 2 * IMG * group + u)
            attend_back(group, u)

        @pl.loop(0, 3)
        def _(n):
            serve(numbers(2 * IMG, 3), 3 * group + n)
            k = 3 * group + n
            produce(base + NO + k, lhs2, lambda half: proj[k, half].reshape(TOK, CW))

        @pl.loop(0, 3)
        def _(n):
            serve(numbers(2 * IMG + 3, 3), 3 * group + n)
            k = 3 * group + n
            wload(base + NO + k).wait()

            @pl.loop(0, 2)
            def _(half):
                acc[...] += dot(proj[k, half].reshape(TOK, CW), wchunk(base + NO + k, half), NT)

            wnext(base + NO + k)

    xs_l.wait()
    serve_next()
    per = SEQ // RB

    def finish(img, row, here):
        at = pl.ds(pl.multiple_of(img * SEQ + row, RB), RB)
        back, product = norm_back(xb[img, pl.ds(row, RB)].astype(F32), acc[at], totals[0:1])
        if here:
            gh[at] = gh[at] + back
        else:
            xb[img, pl.ds(row, RB)] = (gh[at] + back).astype(BF)
        stat[0] += fold(product)

    @pl.loop(0, PIECES)
    def _(n):
        @pl.loop(0, IMG)
        def _(img):
            finish(img, pl.multiple_of(HALF * (1 - x) + PR * n, RB), False)

        piece(1, n).start()

    serve_next()

    @pl.loop(0, PIECES)
    def _(n):
        @pl.loop(0, IMG)
        def _(img):
            finish(img, pl.multiple_of(HALF * x + PR * n, RB), True)

    ig_c = [pltpu.make_async_copy(gh.at[pl.ds(pl.multiple_of(i * SEQ + HALF * x, RB), HALF)], ig_o.at[IMG * x + i],
                                  misc_sem.at[26 + i]) for i in range(IMG)]
    for copy in ig_c:
        copy.start()
    ig_far = [pltpu.make_async_copy(acc.at[pl.ds(i * HALF, HALF)], ig_o.at[IMG * (1 - x) + i], misc_sem.at[28 + i])
              for i in range(IMG)]

    def take_far():
        for n in range(PIECES):
            piece(1, n).wait_recv()

        @pl.loop(0, HALF // RB)
        def _(r):
            row = pl.multiple_of(r * RB, RB)
            for i in range(IMG):
                acc[pl.ds(i * HALF + row, RB)] = igr[i, pl.ds(row, RB)].astype(F32)

        for copy in ig_far:
            copy.start()

    row = lax.broadcasted_iota(jnp.int32, (8, D), 0)
    small = jnp.where(row == 0, jnp.sum(stat[0], axis=0, keepdims=True),
                      jnp.where(row == 1, jnp.sum(stat[1], axis=0, keepdims=True),
                                jnp.tile(loss_i[...], (1, D // 128))))
    steps = (place.over_c(), place.over_y(), place.over_x())

    def small_sum(n):
        if 1 <= n <= 3:
            extra(sbuf.at[2 * n - 2], sbuf.at[2 * n - 1], 1 + n, steps[n - 1]).wait()
        value = small if n == 0 else sbuf[2 * n - 2] + sbuf[2 * n - 1] if n < 4 else None
        if n < 3:
            sbuf[2 * n] = value
            extra(sbuf.at[2 * n], sbuf.at[2 * n + 1], 2 + n, steps[n]).start()
        elif n == 3:
            zsum[z] = value
            for j in range(1, H):
                extra(zsum.at[z], zsum.at[z], 4 + j, place.far(j)).start()
        else:
            for j in range(1, H):
                extra(zsum.at[z], zsum.at[lax.rem(z + H - j, H)], 4 + j, place.far(j)).wait()
            total = jnp.sum(zsum[...], axis=0)
            stat_o[...] = jnp.where(row == 2, total / totals[2:3], total)

    done = [before[i][len(CALLS)] for i in range(5)]
    for n, i in enumerate(DRAIN):
        if n == len(DRAIN) - FAR_AT:
            take_far()
        if i < 4:
            stages[i](jnp.int32(done[i]))
        else:
            small_sum(done[i])
        done[i] += 1
    assert done == [NCH] * 4 + [5] and place_no[0] == len(CALLS)

    for copy in ig_c + ig_far:
        copy.wait()
    for n in range(PIECES):
        piece(0, n).wait_recv()
        piece(1, n).wait_send()

    @pl.loop(NCH - SLOTS, NCH)
    def _(p):
        core_copy(p).wait_send()

    @pl.loop(0, NCH)
    def _(k):
        pltpu.make_async_copy(dw.at[k], do_o.at[:, pl.ds(0, CW)], dw_sem.at[k]).wait()
        for i in range(3):
            near_copy(q.at[k, x, :, yy], k, i, place.over_x()).wait_send()
        for j in range(1, H):
            far_copy(k, z, j).wait_send()


def backward(cfg, saved, mask):
    (wg, at, proj, lse, o, h, bnt, g, gp, gy, gm, gmt, out, xs, ts, totals, loss) = saved
    H, R = cfg["groups"], cfg["rows"]
    NQ, NO, NF = cfg["nq"], cfg["no"], cfg["nf"]
    NCH = NQ + NO + 2 * NF
    IMG, SEQ, D = xs.shape
    TOK = IMG * SEQ
    lhs = (2, D // 2, TOK)
    half = (2, H, 2, R, CW)
    vm = pltpu.VMEM
    dma = pltpu.SemaphoreType.DMA
    return pl.pallas_call(
        functools.partial(bwd_kernel, cfg),
        name="backward_reduce",
        out_shape=[
            jax.ShapeDtypeStruct((2 * IMG, SEQ // 2, D), BF), jax.ShapeDtypeStruct((2 * IMG, SEQ // 2, D), F32),
            jax.ShapeDtypeStruct((3, R, NQ // 3 * CW), F32), jax.ShapeDtypeStruct((R, NO * CW), F32),
            jax.ShapeDtypeStruct((R, NF * CW), F32), jax.ShapeDtypeStruct((R, NF * CW), F32),
            jax.ShapeDtypeStruct((8, D), F32),
        ],
        in_specs=[any_spec()] * 14 + [vmem_spec()] * 3,
        out_specs=[any_spec()] * 6 + [vmem_spec()],
        scratch_shapes=[
            vm((NCH,) + half, BF), vm((SLOTS,) + half, BF), vm((SLOTS,) + half, BF),
            vm((NCH, 3, H, R, CW), BF), vm((NCH, H - 1, R, CW), BF), vm((NCH, R, CW), F32),
            vm((WSLOTS, 2, H, 2, 2, R, CW), BF), vm((2, 2, TOK, CW), BF), vm((2, 2, TOK, CW), BF),
            vm((2, TOK, CW), BF), vm((TOK, CW), F32), vm((TOK, D), BF), vm(lhs, BF), vm(lhs, BF),
            vm((TOK, D), F32), vm((TOK, D), F32), vm((TOK, D), F32), vm(o.shape, BF), vm(o.shape, BF),
            vm(proj.shape, BF), vm(lse.shape, F32), vm(xs.shape, BF),
            vm((IMG, SEQ // 2, D), BF), vm((2, 8, D), F32), vm((6, 8, D), F32), vm((H, 8, D), F32),
            dma((NCH,)), dma((NCH,)), pltpu.SemaphoreType.REGULAR, dma((NCH, 3)), dma((NCH, 3)),
            dma((NCH, H - 1)), dma((NCH, H - 1)), dma((H + 4,)), dma((H + 4,)), dma((2, PIECES)), dma((2, PIECES)),
            dma((NCH,)), dma((NF, 2)), dma((32,)), dma((NCH,)),
        ],
        compiler_params=pltpu.CompilerParams(
            collective_id=1, has_side_effects=True, vmem_limit_bytes=63 * 2**20
        ),
    )(wg, at, proj, lse, o, h, bnt, g, gp, gy, gm, gmt, out, xs, totals, loss, mask)


def per_device(
    inputs, teacher, keep_mask, gain_attn, qkv_weight, out_weight, gain_mlp, up_weight, down_weight
):
    cfg = config(inputs, (qkv_weight, out_weight, up_weight, down_weight))
    R = cfg["rows"]
    saved = forward(
        cfg, inputs, teacher, qkv_weight.transpose(1, 0, 2), out_weight, up_weight, down_weight,
        gain_attn.reshape(1, R), gain_mlp.reshape(1, R), keep_mask
    )
    output, input_grad, qkv_grad, out_grad, up_grad, down_grad, stats = backward(cfg, saved, keep_mask)
    gains = lax.dynamic_slice(stats, (0, lax.axis_index("dp") * R), (2, R))
    return (
        output, stats[2, 0], input_grad, gains[0], qkv_grad.transpose(1, 0, 2), out_grad, gains[1], up_grad, down_grad
    )


def solution(mesh):
    rows = P("dp", "mp", None)
    weight = P("dp", "mp")
    qkv = P("dp", None, "mp")
    return jax.shard_map(
        per_device,
        mesh=mesh,
        in_specs=(rows, rows, P("dp", None), P("dp"), qkv, weight, P("dp"), weight, weight),
        out_specs=(rows, P(), rows, P("dp"), qkv, weight, P("dp"), weight, weight),
        check_vma=False,
    )
```

profile of v0, /device:TPU:0, one launch (start us, length us, event | category | flops | bytes accessed | tf_op | source)
XLA Modules:
  0.0 292.3 jit_solution(15591966715265315814)
XLA Ops:
  0.6 135.5 %gather_forward.1 = (bf16[24,2,4,2,2,64,256]{6,5,4,3,2,1,0:T(8,128)(2,1)}, bf16[2,512,640]{2,1,0:T(8,128)(2,1)}, bf16[6,2,2,320,256]{4,3,2,1,0:T(8,128)(2,1)}, f...) custom-call(bf16[4,160,1024]{2,1,0:T(8,128)(2,1)} %xin.1, ...), custom_call_target="tpu_custom_call" | custom-call | tf_op jit(solution)/shard_map/gather_forward/pallas_call | solution.py:560
  136.2 146.5 %backward_reduce.1 = (bf16[4,160,1024]{2,1,0:T(8,128)(2,1)}, f32[4,160,1024]{2,1,0:T(8,128)}, f32[3,64,512]{2,1,0:T(8,128)}, f32[64,512]{1,0:T(8,128)}, f32[64,2...) custom-call(bf16[24,2,4,2,2,64,256]{6,5,4,3,2,1,0:T(8,128)(2,1)} %get-tuple-element.32.wg, ...), custom_call_target="tpu_custom_call" | custom-call | tf_op jit(solution)/shard_map/backward_reduce/pallas_call | solution.py:1114
  282.7 0.8 constant_dynamic-slice_fusion
  283.5 0.5 slice_bitcast_fusion
  284.0 1.2 slice.9
  285.2 0.0 copy-start
  285.2 2.6 copy.24
  287.8 0.0 copy-done
  287.8 0.0 copy-start.3
  287.8 0.0 copy-start.4
  287.8 1.5 copy.25
  289.3 0.0 copy-done.3
  289.3 0.0 copy-start.2
  289.3 0.0 copy-start.1
  289.3 0.7 copy.26
  290.0 0.0 copy-done.4
  290.0 0.7 copy.27
  290.7 0.0 copy-done.2
  290.7 0.8 copy.28
  291.5 0.0 copy-done.1
  291.5 0.8 copy.29
Async XLA Ops:
  285.2 2.6 copy-start
  287.8 1.5 copy-start.3
  287.8 2.2 copy-start.4
  289.3 1.4 copy-start.2
  289.3 2.2 copy-start.1
where the time goes:
time: 293 us; the launch traced here: 292 us
  Pallas kernels  282 us (96%)
  local copies, waits for them, and re-layouts  9.57 us (3%)
    pallas_call x1, Pallas kernels, backward(): pl.pallas_call(functools.partial(bwd_kernel, cfg), name='backward_reduce'...  146 us
    pallas_call x1, Pallas kernels, forward(): pl.pallas_call(functools.partial(fwd_kernel, cfg), name='gather_forward',...  136 us
    unnamed x16, local copies, waits for them, and re-layouts  7.11 us

commit v1 on v0

--- a/solution.py
+++ b/solution.py
@@ -20,13 +20,13 @@
 FWD_CALLS = (
     (0, 0, 0), (0, 0, 0), (0, 0), (1, 0, 1, 0, 1, 0, 2, 1, 0, 1, 0, 2, 3, 1, 1, 0, 0, 4, 2, 1, 0, 3, 4, 2, 1, 0), (3,), (2,),
     (4, 1), (), (), (), (3, 2, 2, 2, 0), (1, 1, 1),
-    (4, 3, 2, 0, 0, 0), (2, 1), (), (4,), (3, 1, 0, 0, 4), (),
-    (3, 3), (2, 2), (4, 1, 1), (), (4,), (3, 0),
-    (2, 2), (4,), (1, 1), (2, 2, 1, 1, 3, 3, 3, 3, 4), (), (4,),
-    (2,), (4,), (3, 1), (4,), (3,), (4,),
-    (2, 2, 2), (4,), (2, 2, 1, 1), (3, 4), (), (2,),
-    (3,), (3, 2, 3, 4), (3, 4), (3, 4), (3, 4), (4,),
-    (3, 4), (3, 4), (4,),
+    (4, 3, 2, 2, 0, 0, 0), (1, 1), (), (4,), (3, 0, 0, 4), (),
+    (3, 3, 2, 2), (1, 1), (4, 0), (), (4,), (3,),
+    (2, 2), (4,), (1,), (3, 3, 1, 4), (2, 2), (4,),
+    (3, 1), (3, 1, 4), (), (4,), (), (2, 1, 3, 4),
+    (), (3, 2, 2, 2, 2, 2, 1, 1, 4), (), (3, 4), (), (3, 2),
+    (3,), (2, 4), (3, 4), (3, 3, 4), (3, 4), (4,),
+    (4,), (3, 3, 4), (4,),
 )
 NT = (((1,), (1,)), ((), ()))
 NN = (((1,), (0,)), ((), ()))
@@ -234,6 +234,24 @@
     def pieces_in(i):
         for n in range(PIECES):
             piece(i, n, 1 - x).wait_recv()
+
+    def settle(k):
+        keep_chunk(k).wait()
+
+        def late():
+            for j in range(1, H):
+                remote(wg.at[k, :, z, :, c], k, j - 1, place.far(j)).wait_send()
+            for i in (H - 1, H, H + 1):
+                remote(wg.at[k, x, z, yy, c], k, i, place.over_x()).wait_send()
+
+        def early():
+            for j in range(1, H):
+                remote(wg.at[k, x, z, yy, c], k, j - 1, place.far(j)).wait_send()
+            for i in (H - 1, H, H + 1):
+                remote(wg.at[k, x, :, yy, c], k, i, place.over_x()).wait_send()
+
+        either(k, late, early)
+        remote(wg.at[k, :, :, :, c], k, H + 2, place.over_c()).wait_send()
 
     stages = (s1, s2, s3, s4, s5)
     pos = [0] * 5
@@ -321,7 +339,7 @@
     pieces_in(0)
     keep(xs, xs_o)
 
-    RB = 32
+    RB = 64
 
     def rows_of(ref, r):
         per = SEQ // RB
@@ -465,6 +483,11 @@
         def _(half, k=k):
             y[...] += dot(g[k, half], chunk(first_down + k, half), NT)
 
+        if 1 <= k < NF - 1:
+            @pl.loop(3 * k - 3, 3 * k)
+            def _(n):
+                settle(n)
+
     assert pos == [NCH] * 5 and place_no[0] == len(FWD_CALLS)
     tl.wait()
     pieces_in(1)
@@ -512,24 +535,9 @@
     extra(sm.at[:, yy, c], sm.at[:, yy, c], 2, place.over_y()).wait_send()
     extra(sm.at[:, :, c], sm.at[:, :, c], 3, place.over_c()).wait_send()
 
-    @pl.loop(0, NCH)
+    @pl.loop(NCH - 6, NCH)
     def _(k):
-        keep_chunk(k).wait()
-
-        def late():
-            for j in range(1, H):
-                remote(wg.at[k, :, z, :, c], k, j - 1, place.far(j)).wait_send()
-            for i in (H - 1, H, H + 1):
-                remote(wg.at[k, x, z, yy, c], k, i, place.over_x()).wait_send()
-
-        def early():
-            for j in range(1, H):
-                remote(wg.at[k, x, z, yy, c], k, j - 1, place.far(j)).wait_send()
-            for i in (H - 1, H, H + 1):
-                remote(wg.at[k, x, :, yy, c], k, i, place.over_x()).wait_send()
-
-        either(k, late, early)
-        remote(wg.at[k, :, :, :, c], k, H + 2, place.over_c()).wait_send()
+        settle(k)
 
 
 def any_spec():
@@ -598,30 +606,31 @@
 SLOTS = 3
 FAR_AT = 4
 WSLOTS = 4
+BACK_BOTH_X = (0, 4, 5, 10, 12, 15, 18, 23)
+Z_FIRST = (2, 14, 22)
 CALLS = (
-    (0, 0, 0, 0, 0), (0, 0, 0, 0, 0), (0, 0, 0, 0, 0), (1, 0, 0, 0, 0), (0, 0, 0, 0, 0),
-    (1, 0, 0, 0, 0), (0, 0, 0, 0, 0), (1, 0, 0, 0, 0), (0, 1, 0, 0, 0), (1, 0, 0, 0, 0),
-    (0, 1, 0, 0, 0), (1, 0, 0, 0, 0), (0, 0, 0, 0, 0), (1, 0, 0, 0, 0), (0, 1, 0, 0, 0),
-    (1, 0, 0, 0, 0), (0, 0, 0, 0, 0), (1, 0, 0, 0, 0), (0, 0, 2, 0, 0), (1, 1, 1, 0, 0),
-    (1, 0, 0, 0, 0), (0, 0, 0, 0, 0), (0, 0, 0, 0, 0), (1, 1, 0, 1, 0), (0, 0, 0, 0, 0),
-    (1, 0, 0, 1, 0), (0, 0, 0, 0, 0), (1, 1, 1, 1, 0), (1, 0, 0, 0, 0), (0, 1, 0, 0, 0),
-    (0, 0, 0, 0, 0), (1, 1, 0, 0, 0), (1, 0, 0, 1, 0), (0, 1, 1, 0, 0), (0, 1, 0, 0, 0),
-    (0, 0, 0, 0, 0), (0, 0, 0, 0, 0), (1, 0, 0, 0, 0), (0, 1, 0, 0, 0), (1, 0, 3, 1, 0),
-    (0, 1, 3, 0, 0), (0, 1, 0, 1, 0), (0, 1, 1, 1, 0), (0, 0, 0, 0, 0), (0, 0, 1, 1, 0),
-    (0, 1, 0, 0, 0), (1, 0, 0, 1, 0), (1, 0, 1, 0, 0), (1, 1, 0, 1, 0), (0, 1, 1, 1, 0),
-    (0, 0, 1, 1, 0), (0, 1, 1, 1, 0), (0, 1, 0, 2, 0), (0, 0, 0, 0, 0), (0, 1, 1, 1, 0),
-    (0, 0, 0, 0, 0), (1, 0, 0, 1, 0), (1, 0, 1, 0, 0), (1, 1, 1, 0, 0), (0, 1, 0, 1, 0),
+    (0, 0, 0, 0, 0), (0, 0, 0, 0, 0), (1, 0, 0, 0, 0), (0, 0, 0, 0, 0), (1, 0, 0, 0, 0),
+    (0, 0, 0, 0, 0), (1, 1, 0, 0, 0), (0, 0, 0, 0, 0), (1, 0, 0, 0, 0), (0, 1, 0, 0, 0),
+    (1, 0, 0, 0, 0), (0, 0, 0, 0, 0), (1, 0, 0, 0, 0), (0, 0, 1, 0, 0), (1, 0, 1, 0, 0),
+    (0, 0, 0, 0, 0), (1, 0, 0, 0, 0), (0, 3, 0, 0, 0), (1, 0, 0, 0, 0), (0, 0, 0, 1, 0),
+    (1, 1, 0, 0, 0), (0, 0, 0, 1, 0), (1, 0, 0, 0, 0), (0, 1, 0, 0, 0), (1, 0, 0, 0, 0),
+    (0, 0, 0, 0, 0), (1, 0, 0, 0, 0), (0, 1, 0, 0, 0), (1, 0, 0, 0, 0), (0, 0, 2, 0, 0),
+    (1, 0, 0, 0, 0), (0, 0, 1, 0, 0), (1, 1, 0, 0, 0), (0, 0, 2, 0, 0), (0, 1, 1, 0, 0),
+    (0, 0, 0, 2, 0), (1, 0, 0, 0, 0), (0, 0, 1, 0, 0), (0, 0, 0, 0, 0), (1, 1, 0, 0, 0),
+    (0, 1, 0, 0, 0), (0, 0, 1, 1, 0), (0, 1, 2, 2, 0), (0, 2, 0, 0, 0), (0, 0, 0, 1, 0),
+    (1, 1, 0, 0, 0), (1, 0, 1, 1, 0), (1, 0, 0, 0, 0), (0, 0, 1, 1, 0), (0, 1, 0, 1, 0),
+    (0, 1, 0, 1, 0), (0, 0, 3, 1, 0), (0, 1, 1, 2, 0), (0, 1, 0, 0, 0), (0, 0, 0, 0, 0),
+    (1, 0, 0, 1, 0), (1, 1, 1, 0, 0), (1, 0, 1, 1, 0), (0, 1, 0, 1, 0), (0, 0, 1, 1, 0),
 )
 DRAIN = (
-    3, 2, 1, 4, 3, 4, 1, 3, 4, 2, 2, 2, 4, 3, 3, 3, 4,
+    4, 4, 2, 4, 1, 1, 3, 2, 4, 3, 2, 3, 3, 4, 3,
 )
-OUT_FIRST = 1
 
 
 def bwd_kernel(cfg, wg, at_i, proj_i, lse_i, o_i, h_i, bnt_i, g_i, gp_i, gy_i, gm_i, gmt_i, out_i, xs_i,
                totals, loss_i, mask, *refs):
     (out_o, ig_o, dq_o, do_o, du_o, dd_o, stat_o,
-     q, snd, rcv, near, farr, dw, wb, gb_buf, gpb, gz, zb, gm, lhs1, lhs2, acc, gh, h, o, go, proj, lse, xb, igr, stat, sbuf, zsum,
+     q, snd, rcv, near, farr, crossed, dw, wb, gb_buf, gpb, gz, zb, gm, lhs1, lhs2, acc, gh, h, o, go, proj, lse, xb, igr, stat, sbuf, zsum,
      core_send, core_recv, credit, near_send, near_recv, far_send, far_recv, extra_send, extra_recv, piece_send, piece_recv,
      wsem, gsem, misc_sem, dw_sem) = refs
     H, R = cfg["groups"], cfg["rows"]
@@ -640,7 +649,7 @@
         return jnp.where(p < 2 * NF, ff, jnp.where(p < 2 * NF + NO, p - 2 * NF + NQ, p - 2 * NF - NO))
 
     def relay(p):
-        both = (p >= OUT_FIRST) & (p < OUT_FIRST + PIECES)
+        both = member(p, BACK_BOTH_X)
         first = jnp.where(both, 1, 1 - c)
         xa = jnp.where(first == 1, 1 - x, x)
         ya = jnp.where(first == 1, yy, 1 - yy)
@@ -695,6 +704,28 @@
             src, near.at[k, i], near_send.at[k, i], near_recv.at[k, i], device_id=device, device_id_type=MESH
         )
 
+    def crossing(p):
+        slot = jnp.int32(0)
+        for n, number in enumerate(Z_FIRST):
+            slot = jnp.where(p == number, n, slot)
+        return slot
+
+    def cross_copy(p, k, j):
+        return pltpu.make_async_remote_copy(
+            q.at[k, :, lax.rem(z + j, H), :], crossed.at[crossing(p), j - 1], far_send.at[k, j - 1], far_recv.at[k, j - 1],
+            device_id=place.far(j), device_id_type=MESH
+        )
+
+    def single_copy(src, k, i, device):
+        return pltpu.make_async_remote_copy(
+            src, near.at[k, i, 0], near_send.at[k, i], near_recv.at[k, i], device_id=device, device_id_type=MESH
+        )
+
+    def either(p, first, last):
+        crosses = member(p, Z_FIRST)
+        pl.when(crosses)(first)
+        pl.when(jnp.logical_not(crosses))(last)
+
     def far_copy(k, zd, j):
         return pltpu.make_async_remote_copy(
             q.at[k, x, zd, yy], farr.at[k, j - 1], far_send.at[k, j - 1], far_recv.at[k, j - 1],
@@ -730,31 +761,67 @@
         @pl.loop(0, 2 * H)
         def _(n):
             i, m = n // H, lax.rem(n, H)
-            for y2 in range(2):
-                q[k, i, m, y2] = (q[k, i, m, y2].astype(F32) + rcv[s, i, m, y2].astype(F32)).astype(BF)
+            q[k, i, m] = q[k, i, m] + rcv[s, i, m]
 
         pl.when(p + SLOTS < NCH)(
             lambda: pl.semaphore_signal(credit, 1, device_id=place.over_c(), device_id_type=MESH)
         )
         xa, ya, xo, yo = relay(p)
-        near_copy(q.at[k, 1 - x, :, 1 - yy], k, 0, place.at(z, yo, c, xo)).start()
-        near_copy(q.at[k, xo, :, yo], k, 1, place.at(z, yo, c, xo)).start()
+
+        def cross():
+            for j in range(1, H):
+                cross_copy(p, k, j).start()
+
+        def plain():
+            near_copy(q.at[k, 1 - x, :, 1 - yy], k, 0, place.at(z, yo, c, xo)).start()
+            near_copy(q.at[k, xo, :, yo], k, 1, place.at(z, yo, c, xo)).start()
+
+        either(p, cross, plain)
 
     def r2(p):
         k = ident(p)
         xa, ya, xo, yo = relay(p)
-        near_copy(q.at[k, 1 - x, :, 1 - yy], k, 0, place.at(z, yo, c, xo)).wait_recv()
-        added(k, xa, ya, (0,))
-        near_copy(q.at[k, xa, :, ya], k, 2, place.at(z, ya, c, xa)).start()
+
+        def cross():
+            for j in range(1, H):
+                cross_copy(p, k, j).wait_recv()
+            slot = crossing(p)
+
+            @pl.loop(0, 2)
+            def _(i):
+                for m in range(2):
+                    total = q[k, i, z, m].astype(F32)
+                    for j in range(1, H):
+                        total = total + crossed[slot, j - 1, i, m].astype(F32)
+                    q[k, i, z, m] = total.astype(BF)
+
+            single_copy(q.at[k, 1 - x, z, 1 - yy], k, 0, place.at(z, yo, c, xo)).start()
+            single_copy(q.at[k, xo, z, yo], k, 1, place.at(z, yo, c, xo)).start()
+
+        def plain():
+            near_copy(q.at[k, 1 - x, :, 1 - yy], k, 0, place.at(z, yo, c, xo)).wait_recv()
+            added(k, xa, ya, (0,))
+            near_copy(q.at[k, xa, :, ya], k, 2, place.at(z, ya, c, xa)).start()
+
+        either(p, cross, plain)
 
     def r3(p):
         k = ident(p)
         xa, ya, xo, yo = relay(p)
-        near_copy(q.at[k, xo, :, yo], k, 1, place.at(z, yo, c, xo)).wait_recv()
-        near_copy(q.at[k, xa, :, ya], k, 2, place.at(z, ya, c, xa)).wait_recv()
-        added(k, x, yy, (1, 2))
-        for j in range(1, H):
-            far_copy(k, lax.rem(z + j, H), j).start()
+
+        def cross():
+            single_copy(q.at[k, 1 - x, z, 1 - yy], k, 0, place.at(z, yo, c, xo)).wait_recv()
+            q[k, xa, z, ya] = (q[k, xa, z, ya].astype(F32) + near[k, 0, 0].astype(F32)).astype(BF)
+            single_copy(q.at[k, xa, z, ya], k, 2, place.at(z, ya, c, xa)).start()
+
+        def plain():
+            near_copy(q.at[k, xo, :, yo], k, 1, place.at(z, yo, c, xo)).wait_recv()
+            near_copy(q.at[k, xa, :, ya], k, 2, place.at(z, ya, c, xa)).wait_recv()
+            added(k, x, yy, (1, 2))
+            for j in range(1, H):
+                far_copy(k, lax.rem(z + j, H), j).start()
+
+        either(p, cross, plain)
 
     def dw_out(k):
         def send(first, count, at):
@@ -774,11 +841,21 @@
 
     def r4(p):
         k = ident(p)
-        total = q[k, x, z, yy].astype(F32)
-        for j in range(1, H):
-            far_copy(k, lax.rem(z + j, H), j).wait_recv()
-            total = total + farr[k, j - 1].astype(F32)
-        dw[k] = total
+        xa, ya, xo, yo = relay(p)
+
+        def cross():
+            single_copy(q.at[k, xo, z, yo], k, 1, place.at(z, yo, c, xo)).wait_recv()
+            single_copy(q.at[k, xa, z, ya], k, 2, place.at(z, ya, c, xa)).wait_recv()
+            dw[k] = q[k, x, z, yy].astype(F32) + near[k, 1, 0].astype(F32) + near[k, 2, 0].astype(F32)
+
+        def plain():
+            total = q[k, x, z, yy].astype(F32)
+            for j in range(1, H):
+                far_copy(k, lax.rem(z + j, H), j).wait_recv()
+                total = total + farr[k, j - 1].astype(F32)
+            dw[k] = total
+
+        either(p, cross, plain)
         dw_out(k)
 
     stages = (r1, r2, r3, r4)
@@ -885,7 +962,7 @@
         return scaled * (e - first - unit * second), grad * unit
 
     def fold(v):
-        return jnp.sum(v.reshape(RB // 8, 8, D), axis=0)
+        return jnp.sum(v.reshape(-1, 8, D), axis=0)
 
     base = 2 * NF
     stat[...] = jnp.zeros_like(stat)
@@ -893,11 +970,11 @@
     h_l.wait()
 
     for part in range(2):
-        count = TOK // RB // 2
+        count = TOK // GB // 2
 
         @pl.loop(part * count, (part + 1) * count)
         def _(r):
-            at = pl.ds(pl.multiple_of(r * RB, RB), RB)
+            at = pl.ds(pl.multiple_of(r * GB, GB), GB)
             back, product = norm_back(h[at], acc[at], totals[1:2])
             total = gh[at] + back
             gh[at] = total
@@ -1070,10 +1147,33 @@
             total = jnp.sum(zsum[...], axis=0)
             stat_o[...] = jnp.where(row == 2, total / totals[2:3], total)
 
+    def settle(p):
+        k = ident(p)
+        pltpu.make_async_copy(dw.at[k], do_o.at[:, pl.ds(0, CW)], dw_sem.at[k]).wait()
+
+        def cross():
+            for j in range(1, H):
+                cross_copy(p, k, j).wait_send()
+            for i in range(3):
+                single_copy(q.at[k, x, z, yy], k, i, place.over_x()).wait_send()
+
+        def plain():
+            for i in range(3):
+                near_copy(q.at[k, x, :, yy], k, i, place.over_x()).wait_send()
+            for j in range(1, H):
+                far_copy(k, z, j).wait_send()
+
+        either(p, cross, plain)
+
     done = [before[i][len(CALLS)] for i in range(5)]
+    settled = [0]
     for n, i in enumerate(DRAIN):
         if n == len(DRAIN) - FAR_AT:
             take_far()
+        if settled[0] + 2 <= min(done[3], NCH - 6):
+            for p in range(settled[0], settled[0] + 2):
+                settle(jnp.int32(p))
+            settled[0] += 2
         if i < 4:
             stages[i](jnp.int32(done[i]))
         else:
@@ -1091,13 +1191,9 @@
     def _(p):
         core_copy(p).wait_send()
 
-    @pl.loop(0, NCH)
-    def _(k):
-        pltpu.make_async_copy(dw.at[k], do_o.at[:, pl.ds(0, CW)], dw_sem.at[k]).wait()
-        for i in range(3):
-            near_copy(q.at[k, x, :, yy], k, i, place.over_x()).wait_send()
-        for j in range(1, H):
-            far_copy(k, z, j).wait_send()
+    @pl.loop(settled[0], NCH)
+    def _(p):
+        settle(p)
 
 
 def backward(cfg, saved, mask):
@@ -1124,7 +1220,8 @@
         out_specs=[any_spec()] * 6 + [vmem_spec()],
         scratch_shapes=[
             vm((NCH,) + half, BF), vm((SLOTS,) + half, BF), vm((SLOTS,) + half, BF),
-            vm((NCH, 3, H, R, CW), BF), vm((NCH, H - 1, R, CW), BF), vm((NCH, R, CW), F32),
+            vm((NCH, 3, H, R, CW), BF), vm((NCH, H - 1, R, CW), BF),
+            vm((max(len(Z_FIRST), 1), H - 1, 2, 2, R, CW), BF), vm((NCH, R, CW), F32),
             vm((WSLOTS, 2, H, 2, 2, R, CW), BF), vm((2, 2, TOK, CW), BF), vm((2, 2, TOK, CW), BF),
             vm((2, TOK, CW), BF), vm((TOK, CW), F32), vm((TOK, D), BF), vm(lhs, BF), vm(lhs, BF),
             vm((TOK, D), F32), vm((TOK, D), F32), vm((TOK, D), F32), vm(o.shape, BF), vm(o.shape, BF),

time: 293 us -> 283 us (0.966)
  Pallas kernels: 282 us -> 273 us
    pallas_call x1, Pallas kernels: 146 us -> 138 us  [backward(): pl.pallas_call(functools.partial(bwd_kernel, cfg), name='backward_reduce'...]
where the time goes in v1:
time: 283 us
  Pallas kernels  273 us (96%)
  local copies, waits for them, and re-layouts  9.57 us (3%)
    pallas_call x1, Pallas kernels, backward(): pl.pallas_call(functools.partial(bwd_kernel, cfg), name='backward_reduce'...  138 us
    pallas_call x1, Pallas kernels, forward(): pl.pallas_call(functools.partial(fwd_kernel, cfg), name='gather_forward',...  135 us
    unnamed x16, local copies, waits for them, and re-layouts  7.11 us

profile of v1, /device:TPU:0, one launch (start us, length us, event | category | flops | bytes accessed | tf_op | source)
XLA Modules:
  0.0 282.8 jit_solution(12800073490824666155)
XLA Ops:
  0.6 135.0 %gather_forward.1 = (bf16[24,2,4,2,2,64,256]{6,5,4,3,2,1,0:T(8,128)(2,1)}, bf16[2,512,640]{2,1,0:T(8,128)(2,1)}, bf16[6,2,2,320,256]{4,3,2,1,0:T(8,128)(2,1)}, f...) custom-call(bf16[4,160,1024]{2,1,0:T(8,128)(2,1)} %xin.1, ...), custom_call_target="tpu_custom_call" | custom-call | tf_op jit(solution)/shard_map/gather_forward/pallas_call | solution.py:568
  135.6 137.5 %backward_reduce.1 = (bf16[4,160,1024]{2,1,0:T(8,128)(2,1)}, f32[4,160,1024]{2,1,0:T(8,128)}, f32[3,64,512]{2,1,0:T(8,128)}, f32[64,512]{1,0:T(8,128)}, f32[64,2...) custom-call(bf16[24,2,4,2,2,64,256]{6,5,4,3,2,1,0:T(8,128)(2,1)} %get-tuple-element.32.wg, ...), custom_call_target="tpu_custom_call" | custom-call | tf_op jit(solution)/shard_map/backward_reduce/pallas_call | solution.py:1210
  273.2 0.8 constant_dynamic-slice_fusion
  273.9 0.5 slice_bitcast_fusion
  274.5 1.2 slice.9
  275.6 0.0 copy-start
  275.6 2.6 copy.24
  278.3 0.0 copy-done
  278.3 0.0 copy-start.3
  278.3 0.0 copy-start.4
  278.3 1.5 copy.25
  279.8 0.0 copy-done.3
  279.8 0.0 copy-start.2
  279.8 0.0 copy-start.1
  279.8 0.7 copy.26
  280.5 0.0 copy-done.4
  280.5 0.7 copy.27
  281.2 0.0 copy-done.2
  281.2 0.8 copy.28
  282.0 0.0 copy-done.1
  282.0 0.8 copy.29
Async XLA Ops:
  275.6 2.6 copy-start
  278.3 1.5 copy-start.3
  278.3 2.2 copy-start.4
  279.8 1.4 copy-start.2
  279.8 2.2 copy-start.1

commit v2 on v1

--- a/solution.py
+++ b/solution.py
@@ -606,24 +606,24 @@
 SLOTS = 3
 FAR_AT = 4
 WSLOTS = 4
-BACK_BOTH_X = (0, 4, 5, 10, 12, 15, 18, 23)
-Z_FIRST = (2, 14, 22)
+BACK_BOTH_X = (6, 7, 8, 9, 14, 15, 23)
+Z_FIRST = (3, 11, 22)
 CALLS = (
-    (0, 0, 0, 0, 0), (0, 0, 0, 0, 0), (1, 0, 0, 0, 0), (0, 0, 0, 0, 0), (1, 0, 0, 0, 0),
-    (0, 0, 0, 0, 0), (1, 1, 0, 0, 0), (0, 0, 0, 0, 0), (1, 0, 0, 0, 0), (0, 1, 0, 0, 0),
-    (1, 0, 0, 0, 0), (0, 0, 0, 0, 0), (1, 0, 0, 0, 0), (0, 0, 1, 0, 0), (1, 0, 1, 0, 0),
-    (0, 0, 0, 0, 0), (1, 0, 0, 0, 0), (0, 3, 0, 0, 0), (1, 0, 0, 0, 0), (0, 0, 0, 1, 0),
-    (1, 1, 0, 0, 0), (0, 0, 0, 1, 0), (1, 0, 0, 0, 0), (0, 1, 0, 0, 0), (1, 0, 0, 0, 0),
-    (0, 0, 0, 0, 0), (1, 0, 0, 0, 0), (0, 1, 0, 0, 0), (1, 0, 0, 0, 0), (0, 0, 2, 0, 0),
-    (1, 0, 0, 0, 0), (0, 0, 1, 0, 0), (1, 1, 0, 0, 0), (0, 0, 2, 0, 0), (0, 1, 1, 0, 0),
-    (0, 0, 0, 2, 0), (1, 0, 0, 0, 0), (0, 0, 1, 0, 0), (0, 0, 0, 0, 0), (1, 1, 0, 0, 0),
-    (0, 1, 0, 0, 0), (0, 0, 1, 1, 0), (0, 1, 2, 2, 0), (0, 2, 0, 0, 0), (0, 0, 0, 1, 0),
-    (1, 1, 0, 0, 0), (1, 0, 1, 1, 0), (1, 0, 0, 0, 0), (0, 0, 1, 1, 0), (0, 1, 0, 1, 0),
-    (0, 1, 0, 1, 0), (0, 0, 3, 1, 0), (0, 1, 1, 2, 0), (0, 1, 0, 0, 0), (0, 0, 0, 0, 0),
-    (1, 0, 0, 1, 0), (1, 1, 1, 0, 0), (1, 0, 1, 1, 0), (0, 1, 0, 1, 0), (0, 0, 1, 1, 0),
+    (0, 0, 0, 0, 0), (0, 0, 0, 0, 0), (0, 0, 0, 0, 0), (1, 0, 0, 0, 0), (1, 0, 0, 0, 0),
+    (0, 0, 0, 0, 0), (1, 0, 0, 0, 0), (0, 1, 0, 0, 0), (1, 0, 0, 0, 0), (0, 0, 0, 0, 0),
+    (1, 0, 0, 0, 0), (0, 0, 1, 0, 0), (1, 1, 0, 0, 0), (0, 0, 0, 0, 0), (1, 0, 0, 0, 0),
+    (0, 0, 0, 0, 0), (1, 1, 0, 0, 0), (0, 0, 1, 0, 0), (1, 0, 0, 0, 0), (0, 1, 0, 0, 0),
+    (1, 0, 0, 0, 0), (0, 1, 0, 1, 0), (1, 0, 1, 0, 0), (0, 0, 0, 1, 0), (1, 0, 0, 0, 0),
+    (0, 3, 0, 0, 0), (1, 0, 0, 0, 0), (0, 0, 0, 1, 0), (1, 0, 0, 0, 0), (0, 1, 0, 0, 0),
+    (1, 0, 0, 0, 0), (0, 0, 1, 0, 0), (1, 0, 0, 0, 0), (0, 1, 0, 0, 0), (0, 0, 1, 0, 0),
+    (0, 0, 0, 0, 0), (0, 2, 0, 0, 0), (1, 0, 3, 0, 0), (1, 0, 0, 0, 0), (0, 1, 0, 0, 0),
+    (0, 0, 1, 3, 0), (0, 1, 1, 1, 0), (0, 0, 1, 1, 0), (0, 1, 0, 1, 0), (0, 0, 0, 0, 0),
+    (0, 0, 0, 0, 0), (1, 0, 0, 1, 0), (1, 1, 0, 0, 0), (1, 0, 3, 1, 0), (0, 1, 1, 0, 0),
+    (0, 1, 1, 2, 0), (0, 1, 1, 1, 0), (0, 1, 1, 1, 0), (0, 0, 0, 1, 0), (0, 0, 1, 0, 0),
+    (1, 0, 0, 0, 0), (0, 1, 1, 1, 0), (1, 0, 0, 1, 0), (1, 1, 0, 0, 0), (0, 0, 1, 1, 0),
 )
 DRAIN = (
-    4, 4, 2, 4, 1, 1, 3, 2, 4, 3, 2, 3, 3, 4, 3,
+    3, 2, 4, 4, 4, 1, 1, 3, 2, 4, 3, 2, 3, 4, 3,
 )
 
 

time: 283 us -> 282 us (level)
  no operation moved by 1% of the time
where the time goes in v2:
time: 282 us
  Pallas kernels  272 us (96%)
  local copies, waits for them, and re-layouts  9.57 us (3%)
    pallas_call x1, Pallas kernels, backward(): pl.pallas_call(functools.partial(bwd_kernel, cfg), name='backward_reduce'...  137 us
    pallas_call x1, Pallas kernels, forward(): pl.pallas_call(functools.partial(fwd_kernel, cfg), name='gather_forward',...  135 us
    unnamed x16, local copies, waits for them, and re-layouts  7.11 us

profile of v2, /device:TPU:0, one launch (start us, length us, event | category | flops | bytes accessed | tf_op | source)
XLA Modules:
  0.0 281.8 jit_solution(9701899450740823758)
XLA Ops:
  0.6 135.0 %gather_forward.1 = (bf16[24,2,4,2,2,64,256]{6,5,4,3,2,1,0:T(8,128)(2,1)}, bf16[2,512,640]{2,1,0:T(8,128)(2,1)}, bf16[6,2,2,320,256]{4,3,2,1,0:T(8,128)(2,1)}, f...) custom-call(bf16[4,160,1024]{2,1,0:T(8,128)(2,1)} %xin.1, ...), custom_call_target="tpu_custom_call" | custom-call | tf_op jit(solution)/shard_map/gather_forward/pallas_call | solution.py:568
  135.6 136.5 %backward_reduce.1 = (bf16[4,160,1024]{2,1,0:T(8,128)(2,1)}, f32[4,160,1024]{2,1,0:T(8,128)}, f32[3,64,512]{2,1,0:T(8,128)}, f32[64,512]{1,0:T(8,128)}, f32[64,2...) custom-call(bf16[24,2,4,2,2,64,256]{6,5,4,3,2,1,0:T(8,128)(2,1)} %get-tuple-element.32.wg, ...), custom_call_target="tpu_custom_call" | custom-call | tf_op jit(solution)/shard_map/backward_reduce/pallas_call | solution.py:1210
  272.2 0.8 constant_dynamic-slice_fusion
  272.9 0.5 slice_bitcast_fusion
  273.4 1.2 slice.9
  274.6 0.0 copy-start
  274.6 2.6 copy.24
  277.2 0.0 copy-done
  277.3 0.0 copy-start.3
  277.3 0.0 copy-start.4
  277.3 1.5 copy.25
  278.7 0.0 copy-done.3
  278.8 0.0 copy-start.2
  278.8 0.0 copy-start.1
  278.8 0.7 copy.26
  279.5 0.0 copy-done.4
  279.5 0.7 copy.27
  280.2 0.0 copy-done.2
  280.2 0.8 copy.28
  281.0 0.0 copy-done.1
  281.0 0.8 copy.29
Async XLA Ops:
  274.6 2.6 copy-start
  277.3 1.5 copy-start.3
  277.3 2.2 copy-start.4
  278.8 1.4 copy-start.2
  278.8 2.2 copy-start.1

commit v3 on v2

--- a/solution.py
+++ b/solution.py
@@ -13,20 +13,20 @@
 F32 = jnp.float32
 BF = jnp.bfloat16
 PIECES = 5
-BOTH_X = (0, 1, 2, 3, 4, 8, 10, 12, 14, 17)
-Z_LAST = (6, 9, 16)
+BOTH_X = (0, 1, 2, 3, 4, 5, 8, 10, 14, 17, 19)
+Z_LAST = (6, 13, 17)
 X_WITH = (0, 1, 2, 3, 4)
-T_WITH = (10, 12, 14, 15, 17)
+T_WITH = (5, 11, 14, 16, 19)
 FWD_CALLS = (
-    (0, 0, 0), (0, 0, 0), (0, 0), (1, 0, 1, 0, 1, 0, 2, 1, 0, 1, 0, 2, 3, 1, 1, 0, 0, 4, 2, 1, 0, 3, 4, 2, 1, 0), (3,), (2,),
-    (4, 1), (), (), (), (3, 2, 2, 2, 0), (1, 1, 1),
-    (4, 3, 2, 2, 0, 0, 0), (1, 1), (), (4,), (3, 0, 0, 4), (),
-    (3, 3, 2, 2), (1, 1), (4, 0), (), (4,), (3,),
-    (2, 2), (4,), (1,), (3, 3, 1, 4), (2, 2), (4,),
-    (3, 1), (3, 1, 4), (), (4,), (), (2, 1, 3, 4),
-    (), (3, 2, 2, 2, 2, 2, 1, 1, 4), (), (3, 4), (), (3, 2),
-    (3,), (2, 4), (3, 4), (3, 3, 4), (3, 4), (4,),
-    (4,), (3, 3, 4), (4,),
+    (0, 0, 0), (0, 0, 0), (0, 0), (1, 0, 1, 0, 1, 0, 2, 1, 0, 1, 0, 3, 2, 1, 0, 4, 2, 1, 0, 3, 4, 2, 1, 0), (3,), (3, 2),
+    (4, 1), (), (), (), (4, 2, 0), (3, 2, 1),
+    (2, 1, 0), (4, 1, 0), (), (), (3, 2, 2, 1, 1, 0, 0, 0, 4), (),
+    (), (2,), (3, 3, 1), (2, 1, 0, 0, 4), (3, 2, 4), (1,),
+    (4, 3), (), (4, 2), (), (3, 1), (4,),
+    (2, 2), (2, 3, 1, 1, 1, 4), (3,), (4,), (2, 2), (1, 1, 3, 3, 3, 4),
+    (), (4,), (3,), (4,), (), (4,),
+    (), (), (2, 2, 2, 2, 3, 1, 3, 4), (4,), (3, 2, 3, 4), (3, 4),
+    (3, 4), (3, 4), (4,),
 )
 NT = (((1,), (1,)), ((), ()))
 NN = (((1,), (0,)), ((), ()))

time: 282 us -> 282 us (level)
  no operation moved by 1% of the time
where the time goes in v3:
time: 282 us
  Pallas kernels  272 us (96%)
  local copies, waits for them, and re-layouts  9.57 us (3%)
    pallas_call x1, Pallas kernels, backward(): pl.pallas_call(functools.partial(bwd_kernel, cfg), name='backward_reduce'...  136 us
    pallas_call x1, Pallas kernels, forward(): pl.pallas_call(functools.partial(fwd_kernel, cfg), name='gather_forward',...  136 us
    unnamed x16, local copies, waits for them, and re-layouts  7.11 us

profile of v3, /device:TPU:0, one launch (start us, length us, event | category | flops | bytes accessed | tf_op | source)
XLA Modules:
  0.0 282.1 jit_solution(2845580008487135689)
XLA Ops:
  0.6 135.7 %gather_forward.1 = (bf16[24,2,4,2,2,64,256]{6,5,4,3,2,1,0:T(8,128)(2,1)}, bf16[2,512,640]{2,1,0:T(8,128)(2,1)}, bf16[6,2,2,320,256]{4,3,2,1,0:T(8,128)(2,1)}, f...) custom-call(bf16[4,160,1024]{2,1,0:T(8,128)(2,1)} %xin.1, ...), custom_call_target="tpu_custom_call" | custom-call | tf_op jit(solution)/shard_map/gather_forward/pallas_call | solution.py:568
  136.3 136.2 %backward_reduce.1 = (bf16[4,160,1024]{2,1,0:T(8,128)(2,1)}, f32[4,160,1024]{2,1,0:T(8,128)}, f32[3,64,512]{2,1,0:T(8,128)}, f32[64,512]{1,0:T(8,128)}, f32[64,2...) custom-call(bf16[24,2,4,2,2,64,256]{6,5,4,3,2,1,0:T(8,128)(2,1)} %get-tuple-element.32.wg, ...), custom_call_target="tpu_custom_call" | custom-call | tf_op jit(solution)/shard_map/backward_reduce/pallas_call | solution.py:1210
  272.5 0.8 constant_dynamic-slice_fusion
  273.3 0.5 slice_bitcast_fusion
  273.8 1.2 slice.9
  275.0 0.0 copy-start
  275.0 2.6 copy.24
  277.6 0.0 copy-done
  277.6 0.0 copy-start.3
  277.6 0.0 copy-start.4
  277.6 1.5 copy.25
  279.1 0.0 copy-done.3
  279.1 0.0 copy-start.2
  279.1 0.0 copy-start.1
  279.1 0.7 copy.26
  279.8 0.0 copy-done.4
  279.8 0.7 copy.27
  280.5 0.0 copy-done.2
  280.5 0.8 copy.28
  281.3 0.0 copy-done.1
  281.3 0.8 copy.29
Async XLA Ops:
  275.0 2.6 copy-start
  277.6 1.5 copy-start.3
  277.6 2.2 copy-start.4
  279.1 1.4 copy-start.2
  279.1 2.2 copy-start.1
